TPU v7x, 32 devices: a whole 2x2x4 slice. The times are simulated.
32 devices in a mesh: ctx: 4 (over y, x), fsdp: 8 (over z, core).
Axes of the slice: x: 2, y: 2, z: 4, core: 2. Of those that a mesh axis runs over, the one named last changes fastest.
Arguments:
- tokens: bfloat16 [2, 8, 1024, 1024], P(None, 'fsdp', 'ctx'), may hold values from -6 to 6
- doc_lengths: int32 [2, 8, 4], P(None, 'fsdp'), may hold values from 1 to 512, 1024 in all within a row
- w_query: bfloat16 [1024, 1024], P(('ctx', 'fsdp')), may hold values from -0.1875 to 0.1875
- b_query: bfloat16 [1024], P(('ctx', 'fsdp')), may hold values from -1.75 to 1.75
- w_key: bfloat16 [1024, 1024], P(('ctx', 'fsdp')), may hold values from -0.1875 to 0.1875
- w_value: bfloat16 [1024, 1024], P(('ctx', 'fsdp')), may hold values from -0.1875 to 0.1875
- b_value: bfloat16 [1024], P(('ctx', 'fsdp')), may hold values from -0.3125 to 0.3125
- w_out: bfloat16 [1024, 1024], P(('ctx', 'fsdp')), may hold values from -1.5 to 1.5
- b_out: bfloat16 [1024], P(('ctx', 'fsdp')), may hold values from -1.75 to 1.75
- ln1_gain: bfloat16 [1024], P(('ctx', 'fsdp')), may hold values from 0.5 to 1.5
- ln1_bias: bfloat16 [1024], P(('ctx', 'fsdp')), may hold values from -1.75 to 1.75
- w_up: bfloat16 [1024, 4096], P(('ctx', 'fsdp')), may hold values from -0.1875 to 0.1875
- b_up: bfloat16 [4096], P(('ctx', 'fsdp')), may hold values from -1.75 to 1.75
- w_down: bfloat16 [4096, 1024], P(('ctx', 'fsdp')), may hold values from -0.09375 to 0.09375
- b_down: bfloat16 [1024], P(('ctx', 'fsdp')), may hold values from -1.75 to 1.75
- ln2_gain: bfloat16 [1024], P(('ctx', 'fsdp')), may hold values from 0.5 to 1.5
- ln2_bias: bfloat16 [1024], P(('ctx', 'fsdp')), may hold values from -1.75 to 1.75
- cotangent: bfloat16 [2, 8, 1024, 1024], P(None, 'fsdp', 'ctx'), may hold values from -6 to 6
Outputs:
- output: bfloat16 [2, 8, 1024, 1024], P(None, 'fsdp', 'ctx')
- grad_tokens: float32 [2, 8, 1024, 1024], P(None, 'fsdp', 'ctx')
- grad_w_query: float32 [1024, 1024], P(('ctx', 'fsdp'))
- grad_b_query: float32 [1024], P(('ctx', 'fsdp'))
- grad_w_key: float32 [1024, 1024], P(('ctx', 'fsdp'))
- grad_w_value: float32 [1024, 1024], P(('ctx', 'fsdp'))
- grad_b_value: float32 [1024], P(('ctx', 'fsdp'))
- grad_w_out: float32 [1024, 1024], P(('ctx', 'fsdp'))
- grad_b_out: float32 [1024], P(('ctx', 'fsdp'))
- grad_ln1_gain: float32 [1024], P(('ctx', 'fsdp'))
- grad_ln1_bias: float32 [1024], P(('ctx', 'fsdp'))
- grad_w_up: float32 [1024, 4096], P(('ctx', 'fsdp'))
- grad_b_up: float32 [4096], P(('ctx', 'fsdp'))
- grad_w_down: float32 [4096, 1024], P(('ctx', 'fsdp'))
- grad_b_down: float32 [1024], P(('ctx', 'fsdp'))
- grad_ln2_gain: float32 [1024], P(('ctx', 'fsdp'))
- grad_ln2_bias: float32 [1024], P(('ctx', 'fsdp'))
Inputs may be any that keep to these rules, and one draw needn't show every extreme that they name: `doc_lengths`: in each stream the 4 documents fill the 1024 positions in order, and the longest is exactly 512.
All inputs are finite; a program needn't handle non-finite values.
Results may differ from a plain program's by a relative error of at most 0.014.
Values may be sent and summed in bfloat16 or wider, within the bound.
No kernel may reach another device: no remote copies, remote signals or barrier semaphores. Data moves between devices by JAX's collectives and lax.ppermute only.
A program may use at most 256 MiB of HBM per device.

v0:
```python
import jax
import jax.numpy as jnp
from jax import lax
from jax.sharding import PartitionSpec as P

H = 16
HD = 64
EPSILON = 1e-12
SCORE_SCALE = 0.125
MASKED_SCORE = -1e30


def exact_gelu(values_in):
    return jax.nn.gelu(values_in, approximate=False)


def norm_forward(values_in, gain_vec, bias_vec):
    center = values_in - jnp.mean(values_in, axis=-1, keepdims=True)
    inverse = lax.rsqrt(jnp.mean(center * center, axis=-1, keepdims=True) + EPSILON)
    normed = center * inverse
    return (normed * gain_vec + bias_vec, normed, inverse)


def norm_backward(upstream, normed, inverse, gain_vec):
    scaled = upstream * gain_vec
    inner_sum = (
        scaled
        - jnp.mean(scaled, axis=-1, keepdims=True)
        - normed * jnp.mean(scaled * normed, axis=-1, keepdims=True)
    )
    return (inverse * inner_sum, jnp.sum(upstream * normed, axis=0), jnp.sum(upstream, axis=0))


def segment_ids(lengths, positions):
    starts = jnp.cumsum(lengths) - lengths
    return jnp.sum((positions[:, None] >= starts[None, :]).astype(jnp.int32), axis=1) - 1


def to_blocks(stacked):
    streams, row_count, _ = stacked.shape
    pieces = stacked.reshape(streams, row_count, H // 4, 4, HD)
    return jnp.moveaxis(pieces, 2, 1).reshape(streams * (H // 4), row_count, 4, HD)


def from_blocks(stacked, streams):
    _, row_count, heads_block, head_size = stacked.shape
    pieces = stacked.reshape(streams, H // 4, row_count, heads_block, head_size)
    return jnp.moveaxis(pieces, 1, 2).reshape(streams, row_count, H * HD)


def masked_scores(queries, keys_all, seg_rows, seg_cols):
    scores = (
        jnp.einsum("qgd,kgd->gqk", queries, keys_all, preferred_element_type=jnp.float32)
        * SCORE_SCALE
    )
    return jnp.where((seg_rows[:, None] == seg_cols[None, :])[None], scores, MASKED_SCORE)


def attend(operands):
    queries, keys_all, values_all, seg_rows, seg_cols = operands
    scores = masked_scores(queries, keys_all, seg_rows, seg_cols)
    top_score = jnp.max(scores, axis=-1, keepdims=True)
    exponent_terms = jnp.exp(scores - top_score)
    totals = jnp.sum(exponent_terms, axis=-1, keepdims=True)
    probs = exponent_terms / totals
    mixed = jnp.einsum(
        "gqk,kgd->qgd", probs.astype(jnp.bfloat16), values_all, preferred_element_type=jnp.float32
    )
    return (mixed, top_score + jnp.log(totals))


def attend_back(operands):
    queries, keys_all, values_all, seg_rows, seg_cols, log_totals, grad_mixed = operands
    scores = masked_scores(queries, keys_all, seg_rows, seg_cols)
    probs = jnp.exp(scores - log_totals)
    grad_values = jnp.einsum(
        "gqk,qgd->kgd", probs.astype(jnp.bfloat16), grad_mixed, preferred_element_type=jnp.float32
    )
    grad_probs = jnp.einsum(
        "qgd,kgd->gqk", grad_mixed, values_all, preferred_element_type=jnp.float32
    )
    central = jnp.sum(probs * grad_probs, axis=-1, keepdims=True)
    grad_scores = (probs * (grad_probs - central)).astype(jnp.bfloat16)
    grad_queries = (
        jnp.einsum("gqk,kgd->qgd", grad_scores, keys_all, preferred_element_type=jnp.float32)
        * SCORE_SCALE
    )
    grad_keys = (
        jnp.einsum("gqk,qgd->kgd", grad_scores, queries, preferred_element_type=jnp.float32)
        * SCORE_SCALE
    )
    return (grad_queries, grad_keys, grad_values)


def left_product(left, right):
    return jnp.einsum("ta,tb->ab", left, right, preferred_element_type=jnp.float32)


def right_transpose(left, right):
    return jnp.einsum("tb,ab->ta", left, right, preferred_element_type=jnp.float32)


def body(
    tokens,
    doc_lengths,
    w_query,
    b_query,
    w_key,
    w_value,
    b_value,
    w_out,
    b_out,
    ln1_gain,
    ln1_bias,
    w_up,
    b_up,
    w_down,
    b_down,
    ln2_gain,
    ln2_bias,
    cotangent,
):
    micro, per_device, ctx_rows, width = tokens.shape
    stream_len = ctx_rows * lax.axis_size("ctx")
    row_pos = lax.axis_index("ctx") * ctx_rows + jnp.arange(ctx_rows, dtype=jnp.int32)
    key_pos = jnp.arange(stream_len, dtype=jnp.int32)
    blocks_per = H // 4
    flat_rows = per_device * ctx_rows
    outputs = []
    input_grads = []
    accumulated = None
    for batch_index in range(micro):
        full = (
            lax.all_gather(w_query, ("ctx", "fsdp"), axis=0, tiled=True),
            lax.all_gather(b_query, ("ctx", "fsdp"), axis=0, tiled=True),
            lax.all_gather(w_key, ("ctx", "fsdp"), axis=0, tiled=True),
            lax.all_gather(w_value, ("ctx", "fsdp"), axis=0, tiled=True),
            lax.all_gather(b_value, ("ctx", "fsdp"), axis=0, tiled=True),
            lax.all_gather(w_out, ("ctx", "fsdp"), axis=0, tiled=True),
            lax.all_gather(b_out, ("ctx", "fsdp"), axis=0, tiled=True),
            lax.all_gather(ln1_gain, ("ctx", "fsdp"), axis=0, tiled=True),
            lax.all_gather(ln1_bias, ("ctx", "fsdp"), axis=0, tiled=True),
            lax.all_gather(w_up, ("ctx", "fsdp"), axis=0, tiled=True),
            lax.all_gather(b_up, ("ctx", "fsdp"), axis=0, tiled=True),
            lax.all_gather(w_down, ("ctx", "fsdp"), axis=0, tiled=True),
            lax.all_gather(b_down, ("ctx", "fsdp"), axis=0, tiled=True),
            lax.all_gather(ln2_gain, ("ctx", "fsdp"), axis=0, tiled=True),
            lax.all_gather(ln2_bias, ("ctx", "fsdp"), axis=0, tiled=True),
        )
        (
            query_mat,
            query_bias,
            key_mat,
            value_mat,
            value_bias,
            out_mat,
            out_bias,
            gain_one,
            bias_one,
            up_mat,
            up_bias,
            down_mat,
            down_bias,
            gain_two,
            bias_two,
        ) = full
        inputs = tokens[batch_index].reshape(flat_rows, width)
        queries = (
            jnp.dot(inputs, query_mat, preferred_element_type=jnp.float32) + query_bias
        ).astype(jnp.bfloat16)
        keys_mine = jnp.dot(inputs, key_mat, preferred_element_type=jnp.float32).astype(
            jnp.bfloat16
        )
        values_mine = (
            jnp.dot(inputs, value_mat, preferred_element_type=jnp.float32) + value_bias
        ).astype(jnp.bfloat16)
        keys_all, values_all = (
            lax.all_gather(
                keys_mine.reshape(per_device, ctx_rows, width), "ctx", axis=1, tiled=True
            ),
            lax.all_gather(
                values_mine.reshape(per_device, ctx_rows, width), "ctx", axis=1, tiled=True
            ),
        )
        lengths_now = doc_lengths[batch_index]
        seg_rows = jax.vmap(segment_ids, (0, None))(lengths_now, row_pos)
        seg_cols = jax.vmap(segment_ids, (0, None))(lengths_now, key_pos)
        rows_rep = jnp.repeat(seg_rows, blocks_per, axis=0)
        cols_rep = jnp.repeat(seg_cols, blocks_per, axis=0)
        query_blocks = to_blocks(queries.reshape(per_device, ctx_rows, width))
        key_blocks = to_blocks(keys_all)
        value_blocks = to_blocks(values_all)
        mixed_blocks, log_totals = lax.map(
            attend, (query_blocks, key_blocks, value_blocks, rows_rep, cols_rep)
        )
        mixed = from_blocks(mixed_blocks, per_device).reshape(flat_rows, width).astype(jnp.bfloat16)
        attended = jnp.dot(mixed, out_mat, preferred_element_type=jnp.float32) + out_bias
        first, normed_one, inverse_one = norm_forward(
            inputs.astype(jnp.float32) + attended, gain_one, bias_one
        )
        first_low = first.astype(jnp.bfloat16)
        hidden = jnp.dot(first_low, up_mat, preferred_element_type=jnp.float32) + up_bias
        activated_full, gelu_pull = jax.vjp(exact_gelu, hidden)
        activated = activated_full.astype(jnp.bfloat16)
        branch = jnp.dot(activated, down_mat, preferred_element_type=jnp.float32) + down_bias
        result, normed_two, inverse_two = norm_forward(first + branch, gain_two, bias_two)
        outputs.append(result.astype(jnp.bfloat16).reshape(per_device, ctx_rows, width))
        full = (
            lax.all_gather(w_query, ("ctx", "fsdp"), axis=0, tiled=True),
            lax.all_gather(b_query, ("ctx", "fsdp"), axis=0, tiled=True),
            lax.all_gather(w_key, ("ctx", "fsdp"), axis=0, tiled=True),
            lax.all_gather(w_value, ("ctx", "fsdp"), axis=0, tiled=True),
            lax.all_gather(b_value, ("ctx", "fsdp"), axis=0, tiled=True),
            lax.all_gather(w_out, ("ctx", "fsdp"), axis=0, tiled=True),
            lax.all_gather(b_out, ("ctx", "fsdp"), axis=0, tiled=True),
            lax.all_gather(ln1_gain, ("ctx", "fsdp"), axis=0, tiled=True),
            lax.all_gather(ln1_bias, ("ctx", "fsdp"), axis=0, tiled=True),
            lax.all_gather(w_up, ("ctx", "fsdp"), axis=0, tiled=True),
            lax.all_gather(b_up, ("ctx", "fsdp"), axis=0, tiled=True),
            lax.all_gather(w_down, ("ctx", "fsdp"), axis=0, tiled=True),
            lax.all_gather(b_down, ("ctx", "fsdp"), axis=0, tiled=True),
            lax.all_gather(ln2_gain, ("ctx", "fsdp"), axis=0, tiled=True),
            lax.all_gather(ln2_bias, ("ctx", "fsdp"), axis=0, tiled=True),
        )
        (
            query_mat,
            query_bias,
            key_mat,
            value_mat,
            value_bias,
            out_mat,
            out_bias,
            gain_one,
            bias_one,
            up_mat,
            up_bias,
            down_mat,
            down_bias,
            gain_two,
            bias_two,
        ) = full
        upstream = cotangent[batch_index].reshape(flat_rows, width).astype(jnp.float32)
        grad_h2, grad_gain_two, grad_bias_two = norm_backward(
            upstream, normed_two, inverse_two, gain_two
        )
        grad_branch = grad_h2.astype(jnp.bfloat16)
        grad_down_bias = jnp.sum(grad_branch.astype(jnp.float32), axis=0)
        grad_down_mat = left_product(activated, grad_branch)
        grad_activated = right_transpose(grad_branch, down_mat)
        grad_hidden = gelu_pull(grad_activated)[0].astype(jnp.bfloat16)
        grad_up_bias = jnp.sum(grad_hidden.astype(jnp.float32), axis=0)
        grad_up_mat = left_product(first_low, grad_hidden)
        grad_first = right_transpose(grad_hidden, up_mat) + grad_h2
        grad_h1, grad_gain_one, grad_bias_one = norm_backward(
            grad_first, normed_one, inverse_one, gain_one
        )
        grad_attended = grad_h1.astype(jnp.bfloat16)
        grad_out_bias = jnp.sum(grad_attended.astype(jnp.float32), axis=0)
        grad_out_mat = left_product(mixed, grad_attended)
        grad_mixed = right_transpose(grad_attended, out_mat).astype(jnp.bfloat16)
        grad_mixed_blocks = to_blocks(grad_mixed.reshape(per_device, ctx_rows, width))
        grad_query_blocks, grad_key_blocks, grad_value_blocks = lax.map(
            attend_back,
            (
                query_blocks,
                key_blocks,
                value_blocks,
                rows_rep,
                cols_rep,
                log_totals,
                grad_mixed_blocks,
            ),
        )
        grad_keys_all = from_blocks(grad_key_blocks, per_device)
        grad_values_all = from_blocks(grad_value_blocks, per_device)
        grad_keys_mine, grad_values_mine = (
            lax.psum_scatter(
                grad_keys_all.astype(jnp.bfloat16), "ctx", scatter_dimension=1, tiled=True
            ).astype(jnp.float32),
            lax.psum_scatter(
                grad_values_all.astype(jnp.bfloat16), "ctx", scatter_dimension=1, tiled=True
            ).astype(jnp.float32),
        )
        grad_queries = (
            from_blocks(grad_query_blocks, per_device)
            .reshape(flat_rows, width)
            .astype(jnp.bfloat16)
        )
        grad_keys = grad_keys_mine.reshape(flat_rows, width).astype(jnp.bfloat16)
        grad_values = grad_values_mine.reshape(flat_rows, width).astype(jnp.bfloat16)
        grad_query_bias = jnp.sum(grad_queries.astype(jnp.float32), axis=0)
        grad_value_bias = jnp.sum(grad_values.astype(jnp.float32), axis=0)
        grad_query_mat = left_product(inputs, grad_queries)
        grad_key_mat = left_product(inputs, grad_keys)
        grad_value_mat = left_product(inputs, grad_values)
        grad_inputs = (
            grad_h1
            + right_transpose(grad_queries, query_mat)
            + right_transpose(grad_keys, key_mat)
            + right_transpose(grad_values, value_mat)
        )
        input_grads.append(grad_inputs.reshape(per_device, ctx_rows, width))
        owned = (
            lax.psum_scatter(grad_query_mat, ("ctx", "fsdp"), scatter_dimension=0, tiled=True),
            lax.psum_scatter(grad_query_bias, ("ctx", "fsdp"), scatter_dimension=0, tiled=True),
            lax.psum_scatter(grad_key_mat, ("ctx", "fsdp"), scatter_dimension=0, tiled=True),
            lax.psum_scatter(grad_value_mat, ("ctx", "fsdp"), scatter_dimension=0, tiled=True),
            lax.psum_scatter(grad_value_bias, ("ctx", "fsdp"), scatter_dimension=0, tiled=True),
            lax.psum_scatter(grad_out_mat, ("ctx", "fsdp"), scatter_dimension=0, tiled=True),
            lax.psum_scatter(grad_out_bias, ("ctx", "fsdp"), scatter_dimension=0, tiled=True),
            lax.psum_scatter(grad_gain_one, ("ctx", "fsdp"), scatter_dimension=0, tiled=True),
            lax.psum_scatter(grad_bias_one, ("ctx", "fsdp"), scatter_dimension=0, tiled=True),
            lax.psum_scatter(grad_up_mat, ("ctx", "fsdp"), scatter_dimension=0, tiled=True),
            lax.psum_scatter(grad_up_bias, ("ctx", "fsdp"), scatter_dimension=0, tiled=True),
            lax.psum_scatter(grad_down_mat, ("ctx", "fsdp"), scatter_dimension=0, tiled=True),
            lax.psum_scatter(grad_down_bias, ("ctx", "fsdp"), scatter_dimension=0, tiled=True),
            lax.psum_scatter(grad_gain_two, ("ctx", "fsdp"), scatter_dimension=0, tiled=True),
            lax.psum_scatter(grad_bias_two, ("ctx", "fsdp"), scatter_dimension=0, tiled=True),
        )
        accumulated = owned if accumulated is None else jax.tree.map(jnp.add, accumulated, owned)
    stacked_out = jnp.stack(outputs)
    stacked_grads = jnp.stack(input_grads)
    return (
        stacked_out,
        stacked_grads,
        accumulated[0],
        accumulated[1],
        accumulated[2],
        accumulated[3],
        accumulated[4],
        accumulated[5],
        accumulated[6],
        accumulated[7],
        accumulated[8],
        accumulated[9],
        accumulated[10],
        accumulated[11],
        accumulated[12],
        accumulated[13],
        accumulated[14],
    )


def solution(mesh):
    placed = (
        P(None, "fsdp", "ctx", None),
        P(None, "fsdp", None),
        P(("ctx", "fsdp"), None),
        P(("ctx", "fsdp")),
        P(("ctx", "fsdp"), None),
        P(("ctx", "fsdp"), None),
        P(("ctx", "fsdp")),
        P(("ctx", "fsdp"), None),
        P(("ctx", "fsdp")),
        P(("ctx", "fsdp")),
        P(("ctx", "fsdp")),
        P(("ctx", "fsdp"), None),
        P(("ctx", "fsdp")),
        P(("ctx", "fsdp"), None),
        P(("ctx", "fsdp")),
        P(("ctx", "fsdp")),
        P(("ctx", "fsdp")),
        P(None, "fsdp", "ctx", None),
    )
    return jax.shard_map(
        body,
        mesh=mesh,
        in_specs=placed,
        out_specs=(
            P(None, "fsdp", "ctx", None),
            P(None, "fsdp", "ctx", None),
            P(("ctx", "fsdp"), None),
            P(("ctx", "fsdp")),
            P(("ctx", "fsdp"), None),
            P(("ctx", "fsdp"), None),
            P(("ctx", "fsdp")),
            P(("ctx", "fsdp"), None),
            P(("ctx", "fsdp")),
            P(("ctx", "fsdp")),
            P(("ctx", "fsdp")),
            P(("ctx", "fsdp"), None),
            P(("ctx", "fsdp")),
            P(("ctx", "fsdp"), None),
            P(("ctx", "fsdp")),
            P(("ctx", "fsdp")),
            P(("ctx", "fsdp")),
        ),
        check_vma=False,
    )
```

profile of v0, /device:TPU:0, one launch (start us, length us, event | category | flops | bytes accessed | tf_op | source)
XLA Modules:
  0.0 1791.1 jit_solution(13232261122871129861)
XLA Ops:
  16.2 42.3 %all-reduce.18 = (bf16[1024]{0:T(1024)(128)(2,1)S(1)}, bf16[1024]{0:T(1024)(128)(2,1)S(1)}, bf16[1024]{0:T(1024)(128)(2,1)S(1)}, bf16[1024]{0:T(1024)(128)(2,1)S...) all-reduce(bf16[1024]{0:T(1024)(128)(2,1)S(1)} %dynamic-update-slic, ...), channel_id=1, replica_groups=mesh['ctx'=4,'fsdp'=8] {'ctx','fsdp'}, use_global_device_ids=true, to_apply=%add | all-reduce | flops 8192 | bytes 32768
  58.5 11.8 all-gather.16.cloned.1.call-done
  73.7 55.0 %all-gather.20.cloned.1.call-done = bf16[1024,1024]{1,0:T(8,128)(2,1)} async-done(((bf16[32,1024]{1,0:T(8,128)(2,1)}), bf16[1024,1024]{1,0:T(8,128)(2,1)}) %all-gather.20.cloned.1.call-update) | async-done | bytes 2097168 | tf_op jit(solution)/shard_map/all_gather | solution.py:136
  138.8 39.2 %all-gather.4 = bf16[32,1,128]{2,1,0:T(2,128)(2,1)S(1)} all-gather(bf16[1,1,128]{2,1,0:T(2,128)(2,1)S(1)} %bitcast.493), channel_id=1, replica_groups=mesh['ctx'=4,'fsdp'=8] {'ctx','fsdp'}, dimensions={0}, use_global_device_ids=true | all-gather | bytes 8448 | tf_op jit(solution)/shard_map/all_gather | solution.py:144
  196.0 27.7 %all-gather.28.cloned.1.call-done = bf16[1024,1024]{1,0:T(8,128)(2,1)} async-done(((bf16[256,1024]{1,0:T(8,128)(2,1)}), bf16[1024,1024]{1,0:T(8,128)(2,1)}) %all-gather.28.cloned.1.call-update) | async-done | bytes 2097168 | tf_op jit(solution)/shard_map/all_gather | solution.py:181
  228.0 33.2 %all-gather.30.cloned.1.call-done = bf16[1024,1024]{1,0:T(8,128)(2,1)} async-done(((bf16[256,1024]{1,0:T(8,128)(2,1)}), bf16[1024,1024]{1,0:T(8,128)(2,1)}) %all-gather.30.cloned.1.call-update) | async-done | bytes 2097168 | tf_op jit(solution)/shard_map/all_gather | solution.py:178
  265.0 26.7 %while.52 = (s32[]{:T(128)}, bf16[4,256,4,64]{1,3,2,0:T(8,128)(2,1)}, f32[4,4,256,1]{2,1,3,0:T(4,128)S(1)}, bf16[4,1024,4,64]{1,3,2,0:T(8,128)(2,1)}, s32[4,256]...) while((s32[]{:T(128)}, ...), condition=%wide.region_6.7_spmd, body=%wide.region_3.6_spmd.sunk | while | flops 281279488 | bytes 19317928 | solution.py:193
  302.2 33.2 %all-gather.34.cloned.1.call-done = bf16[1024,1024]{1,0:T(8,128)(2,1)} async-done(((bf16[256,1024]{1,0:T(8,128)(2,1)}), bf16[1024,1024]{1,0:T(8,128)(2,1)}) %all-gather.34.cloned.1.call-update) | async-done | bytes 2097168 | tf_op jit(solution)/shard_map/all_gather | solution.py:178
  338.4 56.6 %all-gather.22.cloned.1.call-done = bf16[1024,1024]{1,0:T(8,128)(2,1)} async-done(((bf16[32,1024]{1,0:T(8,128)(2,1)}), bf16[1024,1024]{1,0:T(8,128)(2,1)}) %all-gather.22.cloned.1.call-update) | async-done | bytes 2097168 | tf_op jit(solution)/shard_map/all_gather | solution.py:139
  398.9 23.4 %while.53 = (s32[]{:T(128)}, bf16[4,256,4,64]{1,3,2,0:T(8,128)(2,1)S(1)}, f32[4,4,256,1]{2,1,3,0:T(4,128)S(1)}, bf16[4,1024,4,64]{1,3,2,0:T(8,128)(2,1)}, s32[4,...) while((s32[]{:T(128)}, ...), condition=%wide.region_17.18_spmd, body=%wide.region_14.17_spmd.sunk | while | flops 281279488 | bytes 15123569 | solution.py:193
  426.4 47.9 %all-gather.24.cloned.1.call-done = bf16[1024,4096]{1,0:T(8,128)(2,1)} async-done(((bf16[32,4096]{1,0:T(8,128)(2,1)}), bf16[1024,4096]{1,0:T(8,128)(2,1)}) %all-gather.24.cloned.1.call-update) | async-done | bytes 8388624 | tf_op jit(solution)/shard_map/all_gather | solution.py:143
  474.3 16.4 multiply_convert_fusion.3
  490.7 62.5 %all-gather.26.cloned.1.call-done = bf16[4096,1024]{1,0:T(8,128)(2,1)} async-done(((bf16[128,1024]{1,0:T(8,128)(2,1)}), bf16[4096,1024]{1,0:T(8,128)(2,1)}) %all-gather.26.cloned.1.call-update) | async-done | bytes 8388624 | tf_op jit(solution)/shard_map/all_gather | solution.py:145
  560.3 13.4 multiply_convert_fusion.2
  580.6 13.1 convert_reduce_fusion.1
  593.7 7.4 multiply_reduce_fusion.3
  601.2 11.9 convert_reduce_fusion
  613.0 8.6 convert_reduce_fusion.7
  632.5 45.7 %while.54 = (s32[]{:T(128)}, bf16[4,256,4,64]{1,3,2,0:T(8,128)(2,1)S(1)}, bf16[4,1024,4,64]{1,3,2,0:T(8,128)(2,1)}, bf16[4,1024,4,64]{1,3,2,0:T(8,128)(2,1)}, bf...) while((s32[]{:T(128)}, ...), condition=%wide.region_28.29_spmd, body=%wide.region_26.28_spmd.sunk | while | flops 687406080 | bytes 72663312 | solution.py:262
  682.3 45.9 %while.55 = (s32[]{:T(128)}, bf16[4,256,4,64]{1,3,2,0:T(8,128)(2,1)}, bf16[4,1024,4,64]{1,3,2,0:T(8,128)(2,1)}, bf16[4,1024,4,64]{1,3,2,0:T(8,128)(2,1)}, bf16[4...) while((s32[]{:T(128)}, ...), condition=%wide.region_37.38_spmd, body=%wide.region_35.37_spmd.sunk | while | flops 687406080 | bytes 76857680 | solution.py:262
  747.7 14.6 reduce-scatter.21.cloned.1.call-done
  772.7 27.8 %reduce-scatter.19.cloned.1.call-done = bf16[1,256,1024]{1,2,0:T(8,128)(2,1)} async-done(((bf16[1,1024,1024]{1,2,0:T(8,128)(2,1)}), bf16[1,256,1024]{1,2,0:T(8,128)(2,1)}) %reduce-scatter.19.cloned.1.call-update) | async-done | bytes 524304 | tf_op jit(solution)/shard_map/reduce_scatter | solution.py:280
  804.2 34.6 %reduce-scatter.23.cloned.1.call-done = bf16[1,256,1024]{1,2,0:T(8,128)(2,1)} async-done(((bf16[1,1024,1024]{1,2,0:T(8,128)(2,1)}), bf16[1,256,1024]{1,2,0:T(8,128)(2,1)}) %reduce-scatter.23.cloned.1.call-update) | async-done | bytes 524304 | tf_op jit(solution)/shard_map/reduce_scatter | solution.py:280
  854.3 10.0 convolution_add_fusion.1
  869.5 10.1 convolution_add_fusion
  892.6 40.6 %all-reduce.17 = (f32[1024]{0:T(1024)S(1)}, f32[1024]{0:T(1024)S(1)}, f32[1024]{0:T(1024)S(1)}, f32[1024]{0:T(1024)S(1)}, f32[1024]{0:T(1024)S(1)}, /*index=5*/f...) all-reduce(f32[1024]{0:T(1024)S(1)} %reshape.711, ...), channel_id=26, replica_groups=mesh['ctx'=4,'fsdp'=8] {'ctx','fsdp'}, use_global_device_ids=true, to_apply=%region_43.44.clone | all-reduce | flops 12288 | bytes 98304
  945.3 39.1 %reduce-scatter.31.cloned.1.call-done = f32[32,1024]{1,0:T(8,128)} async-done(((f32[1024,1024]{1,0:T(8,128)}), f32[32,1024]{1,0:T(8,128)}) %reduce-scatter.31.cloned.1.call-update) | async-done | bytes 131088
  984.3 142.3 %reduce-scatter.25.cloned.1.call-done = f32[32,1024]{1,0:T(8,128)} async-done(((f32[1024,1024]{1,0:T(8,128)}), f32[32,1024]{1,0:T(8,128)}) %reduce-scatter.25.cloned.1.call-update) | async-done | bytes 131088 | tf_op jit(solution)/shard_map/reduce_scatter | solution.py:309
  1126.6 141.8 %reduce-scatter.33.cloned.1.call-done = f32[32,1024]{1,0:T(8,128)} async-done(((f32[1024,1024]{1,0:T(8,128)}), f32[32,1024]{1,0:T(8,128)}) %reduce-scatter.33.cloned.1.call-update) | async-done | bytes 131088
  1268.4 142.2 %reduce-scatter.35.cloned.1.call-done = f32[32,1024]{1,0:T(8,128)} async-done(((f32[1024,1024]{1,0:T(8,128)}), f32[32,1024]{1,0:T(8,128)}) %reduce-scatter.35.cloned.1.call-update) | async-done | bytes 131088
  1410.6 186.4 %reduce-scatter.27.cloned.1.call-done = f32[32,4096]{1,0:T(8,128)} async-done(((f32[1024,4096]{1,0:T(8,128)}), f32[32,4096]{1,0:T(8,128)}) %reduce-scatter.27.cloned.1.call-update) | async-done | bytes 524304 | tf_op jit(solution)/shard_map/reduce_scatter | solution.py:313
  1597.0 187.1 %reduce-scatter.29.cloned.1.call-done = f32[128,1024]{1,0:T(8,128)} async-done(((f32[4096,1024]{1,0:T(8,128)}), f32[128,1024]{1,0:T(8,128)}) %reduce-scatter.29.cloned.1.call-update) | async-done | bytes 524304 | tf_op jit(solution)/shard_map/reduce_scatter | solution.py:315
  (580 shorter events, 317.4 us)
Async XLA Ops:
  7.2 121.6 %copy-start.7 = (bf16[2,1,256,1024]{3,2,1,0:T(8,128)(2,1)S(1)}, bf16[2,1,256,1024]{3,2,1,0:T(8,128)(2,1)}, u32[]{:S(2)}) copy-start(bf16[2,1,256,1024]{3,2,1,0:T(8,128)(2,1)} %param.26) | copy-start | bytes 3145732
  7.2 63.0 %all-gather.16.cloned.1.call-start = ((), (), s32[]{:S(2)}) async-start(), calls=%async_computation.10 | async-start | bytes 2162688 | tf_op jit(solution)/shard_map/all_gather | solution.py:137
  7.9 120.8 %all-gather.20.cloned.1.call-start = ((), (), s32[]{:S(2)}) async-start(), calls=%async_computation.12 | async-start | bytes 2162688 | tf_op jit(solution)/shard_map/all_gather | solution.py:136
  8.7 178.4 %all-gather.18.cloned.1.call-start = ((), (), s32[]{:S(2)}) async-start(), calls=%async_computation.11 | async-start | bytes 2162688 | tf_op jit(solution)/shard_map/all_gather | solution.py:134
  9.4 214.2 %all-gather.28.cloned.1.call-start = ((), (), s32[]{:S(2)}) async-start(), calls=%async_computation.20 | async-start | bytes 2621440 | tf_op jit(solution)/shard_map/all_gather | solution.py:181
  70.2 61.7 %copy-start.22 = (bf16[1024,1024]{1,0:T(8,128)(2,1)S(1)}, bf16[1024,1024]{1,0:T(8,128)(2,1)}, u32[]{:S(2)}) copy-start(bf16[1024,1024]{1,0:T(8,128)(2,1)} %all-gather.16.cloned.1.call-done) | copy-start | bytes 6291460
  73.7 187.6 %all-gather.30.cloned.1.call-start = ((), (), s32[]{:S(2)}) async-start(), calls=%async_computation.21 | async-start | bytes 2621440 | tf_op jit(solution)/shard_map/all_gather | solution.py:178
  131.9 166.4 %all-gather.32.cloned.1.call-start = ((), (), s32[]{:S(2)}) async-start(), calls=%async_computation.22 | async-start | bytes 2621440 | tf_op jit(solution)/shard_map/all_gather | solution.py:181
  133.5 202.0 %all-gather.34.cloned.1.call-start = ((), (), s32[]{:S(2)}) async-start(), calls=%async_computation.23 | async-start | bytes 2621440 | tf_op jit(solution)/shard_map/all_gather | solution.py:178
  136.6 258.3 %all-gather.22.cloned.1.call-start = ((), (), s32[]{:S(2)}) async-start(), calls=%async_computation.13 | async-start | bytes 2162688 | tf_op jit(solution)/shard_map/all_gather | solution.py:139
  137.4 336.9 %all-gather.24.cloned.1.call-start = ((), (), s32[]{:S(2)}) async-start(), calls=%async_computation.14 | async-start | bytes 8650752 | tf_op jit(solution)/shard_map/all_gather | solution.py:143
  138.1 415.1 %all-gather.26.cloned.1.call-start = ((), (), s32[]{:S(2)}) async-start(), calls=%async_computation.15 | async-start | bytes 8650752 | tf_op jit(solution)/shard_map/all_gather | solution.py:145
  138.7 605.3 %reduce-scatter.17.cloned.1.call-start = ((), (), s32[]{:S(2)}) async-start(), calls=%async_computation.16 | async-start | bytes 2621440 | tf_op jit(solution)/shard_map/reduce_scatter | solution.py:277
  178.7 395.0 %copy-start.53 = (f32[1024]{0:T(1024)}, f32[1024]{0:T(1024)S(1)}, u32[]{:S(2)}) copy-start(f32[1024]{0:T(1024)S(1)} %convert_element_type.386) | copy-start | bytes 12292
  422.3 68.4 %copy-start = (bf16[4,1024,4,64]{1,3,2,0:T(8,128)(2,1)}, bf16[4,1024,4,64]{1,3,2,0:T(8,128)(2,1)S(1)}, u32[]{:S(2)}) copy-start(bf16[4,1024,4,64]{1,3,2,0:T(8,128)(2,1)S(1)} %get-tuple-element.861) | copy-start | bytes 6291460
  422.3 68.4 %copy-start.55 = (s32[4,1024]{1,0:T(4,128)}, s32[4,1024]{1,0:T(4,128)S(1)}, u32[]{:S(2)}) copy-start(s32[4,1024]{1,0:T(4,128)S(1)} %get-tuple-element.907) | copy-start | bytes 49156
  422.3 68.4 %copy-start.58 = (f32[4,4,256,1]{2,1,3,0:T(4,128)}, f32[4,4,256,1]{2,1,3,0:T(4,128)S(1)}, u32[]{:S(2)}) copy-start(f32[4,4,256,1]{2,1,3,0:T(4,128)S(1)} %get-tuple-element.773) | copy-start | bytes 49156
  422.3 68.4 %copy-start.59 = (s32[4,256]{1,0:T(4,128)}, s32[4,256]{1,0:T(4,128)S(1)}, u32[]{:S(2)}) copy-start(s32[4,256]{1,0:T(4,128)S(1)} %get-tuple-element.917) | copy-start | bytes 12292
  426.1 195.6 %copy-start.5 = (f32[256,1024]{1,0:T(8,128)}, f32[256,1024]{1,0:T(8,128)S(1)}, u32[]{:S(2)}) copy-start(f32[256,1024]{1,0:T(8,128)S(1)} %get-tuple-element.451) | copy-start | bytes 3145732
  426.1 195.6 %copy-start.62 = (f32[256]{0:T(256)}, f32[256]{0:T(256)S(1)}, u32[]{:S(2)}) copy-start(f32[256]{0:T(256)S(1)} %broadcast_multiply_fusion.9) | copy-start | bytes 3076
  426.4 195.3 %copy-start.64 = (f32[256]{0:T(256)}, f32[256]{0:T(256)S(1)}, u32[]{:S(2)}) copy-start(f32[256]{0:T(256)S(1)} %add_rsqrt_fusion.1) | copy-start | bytes 3076
  678.2 84.1 %reduce-scatter.21.cloned.1.call-start = ((), (), s32[]{:S(2)}) async-start(), calls=%async_computation.18 | async-start | bytes 2621440 | tf_op jit(solution)/shard_map/reduce_scatter | solution.py:277
  728.2 72.3 %reduce-scatter.19.cloned.1.call-start = ((), (), s32[]{:S(2)}) async-start(), calls=%async_computation.17 | async-start | bytes 2621440 | tf_op jit(solution)/shard_map/reduce_scatter | solution.py:280
  728.9 109.9 %reduce-scatter.23.cloned.1.call-start = ((), (), s32[]{:S(2)}) async-start(), calls=%async_computation.19 | async-start | bytes 2621440 | tf_op jit(solution)/shard_map/reduce_scatter | solution.py:280
  729.5 254.8 %reduce-scatter.31.cloned.1.call-start = ((), (), s32[]{:S(2)}) async-start(), calls=%async_computation.27 | async-start | bytes 4325376
  738.8 387.8 %reduce-scatter.25.cloned.1.call-start = ((), (), s32[]{:S(2)}) async-start(), calls=%async_computation.24 | async-start | bytes 4325376 | tf_op jit(solution)/shard_map/reduce_scatter | solution.py:309
  743.9 524.5 %reduce-scatter.33.cloned.1.call-start = ((), (), s32[]{:S(2)}) async-start(), calls=%async_computation.28 | async-start | bytes 4325376
  772.7 637.9 %reduce-scatter.35.cloned.1.call-start = ((), (), s32[]{:S(2)}) async-start(), calls=%async_computation.29 | async-start | bytes 4325376
  849.3 747.7 %reduce-scatter.27.cloned.1.call-start = ((), (), s32[]{:S(2)}) async-start(), calls=%async_computation.25 | async-start | bytes 17301504 | tf_op jit(solution)/shard_map/reduce_scatter | solution.py:313
  864.3 919.8 %reduce-scatter.29.cloned.1.call-start = ((), (), s32[]{:S(2)}) async-start(), calls=%async_computation.26 | async-start | bytes 17301504 | tf_op jit(solution)/shard_map/reduce_scatter | solution.py:315
  890.4 51.1 %copy-start.39 = (bf16[1,256,1024]{1,2,0:T(8,128)(2,1)S(1)}, bf16[1,256,1024]{1,2,0:T(8,128)(2,1)}, u32[]{:S(2)}) copy-start(bf16[1,256,1024]{1,2,0:T(8,128)(2,1)} %reduce-scatter.23.cloned.1.call-done) | copy-start | bytes 1572868
  892.1 49.3 %copy-start.23 = (bf16[1024,1024]{1,0:T(8,128)(2,1)S(1)}, bf16[1024,1024]{1,0:T(8,128)(2,1)}, u32[]{:S(2)}) copy-start(bf16[1024,1024]{1,0:T(8,128)(2,1)} %all-gather.16.cloned.1.call-done) | copy-start | bytes 6291460
  (119 other events, 599.0 us)
Sparse Core Ops, SparseCore 0:
  11.0 59.1 all-gather.15
  73.2 55.4 all-gather.19
  131.7 55.3 all-gather.17
  189.4 34.2 all-gather.27
  225.9 35.2 all-gather.29
  263.0 35.2 all-gather.31
  300.2 35.2 all-gather.33
  338.5 56.4 all-gather.21
  398.0 76.2 all-gather.23
  477.1 76.0 all-gather.25
  678.3 33.7 reduce-scatter.16
  728.3 33.9 reduce-scatter.20
  765.3 35.1 reduce-scatter.18
  803.6 35.1 reduce-scatter.22
  841.5 142.7 reduce-scatter.30
  987.0 139.5 reduce-scatter.24
  1129.3 139.0 reduce-scatter.32
  1271.1 139.4 reduce-scatter.34
  1413.5 183.4 reduce-scatter.26
  1599.7 184.3 reduce-scatter.28
where the time goes:
time: 1800 us; the launch traced here: 1790 us
  waiting for transfers between devices  1260 us (70%)
  matrix products  253 us (14%)
  blocking collectives  122 us (7%)
  local copies, waits for them, and re-layouts  96.3 us (5%)
  other arithmetic  39.1 us (2%)
    unnamed x23, waiting for transfers between devices  328 us
    reduce_scatter x1, waiting for transfers between devices, body(): lax.psum_scatter(grad_down_mat, ('ctx', 'fsdp'), scatter_dimension=0, til...  187 us
    reduce_scatter x1, waiting for transfers between devices, body(): lax.psum_scatter(grad_up_mat, ('ctx', 'fsdp'), scatter_dimension=0, tiled...  186 us
    reduce_scatter x1, waiting for transfers between devices, body(): lax.psum_scatter(grad_out_mat, ('ctx', 'fsdp'), scatter_dimension=0, tile...  142 us
    unnamed x2, blocking collectives  82.9 us
    all_gather x2, waiting for transfers between devices, body(): lax.all_gather(keys_mine.reshape(per_device, ctx_rows, width), 'ctx', axi...  66.5 us
    all_gather x1, waiting for transfers between devices, body(): lax.all_gather(w_down, ('ctx', 'fsdp'), axis=0, tiled=True)  62.5 us
    reduce_scatter x2, waiting for transfers between devices, body(): lax.psum_scatter(grad_values_all.astype(jnp.bfloat16), 'ctx', scatter_dim...  62.4 us
  transfers between devices with their start and end apart: 20, of which 19 were waited for; matrix products, arithmetic and copies ran while one was open for 14% of the time, Pallas kernels for 0%

commit v1 on v0

--- a/solution.py
+++ b/solution.py
@@ -1,3 +1,4 @@
+import functools
 import jax
 import jax.numpy as jnp
 from jax import lax
@@ -8,6 +9,23 @@
 EPSILON = 1e-12
 SCORE_SCALE = 0.125
 MASKED_SCORE = -1e30
+
+
+def track_joints(buf, comm_axis):
+    small, u_next = (lax.psum(1, comm_axis), lax.axis_index(comm_axis))
+    out_arr, prior = (buf, 1)
+    while prior < small:
+        z_new = lax.ppermute(
+            out_arr, comm_axis, tuple(((num, num ^ prior) for num in range(small)))
+        )
+        block_last = jnp.concatenate([out_arr, z_new], axis=0)
+        earlier = jnp.concatenate([z_new, out_arr], axis=0)
+        out_arr = jnp.where(u_next & prior == 0, block_last, earlier)
+        prior = 2 * prior
+    return out_arr
+
+
+entries_lay = functools.partial(track_joints, comm_axis=("ctx", "fsdp"))
 
 
 def exact_gelu(values_in):
@@ -140,7 +158,7 @@
             lax.all_gather(b_out, ("ctx", "fsdp"), axis=0, tiled=True),
             lax.all_gather(ln1_gain, ("ctx", "fsdp"), axis=0, tiled=True),
             lax.all_gather(ln1_bias, ("ctx", "fsdp"), axis=0, tiled=True),
-            lax.all_gather(w_up, ("ctx", "fsdp"), axis=0, tiled=True),
+            entries_lay(w_up),
             lax.all_gather(b_up, ("ctx", "fsdp"), axis=0, tiled=True),
             lax.all_gather(w_down, ("ctx", "fsdp"), axis=0, tiled=True),
             lax.all_gather(b_down, ("ctx", "fsdp"), axis=0, tiled=True),

time: 1800 us -> 1850 us (1.028)
  waiting for transfers between devices: 1260 us -> 1300 us
    ppermute x0 -> x5, waiting for transfers between devices: none -> 86.7 us  [track_joints(): lax.ppermute(out_arr, comm_axis, tuple(((num, num ^ prior) for num in ran...]
    all_gather x1, waiting for transfers between devices: 56.6 us -> 28.8 us  [body(): lax.all_gather(w_out, ('ctx', 'fsdp'), axis=0, tiled=True)]
    all_gather x1, waiting for transfers between devices: 62.5 us -> 42.5 us  [body(): lax.all_gather(w_down, ('ctx', 'fsdp'), axis=0, tiled=True)]
  transfers between devices with their start and end apart: 20 -> 25, of which waited for: 19 -> 21; matrix products, arithmetic and copies ran while one was open for 14% -> 16% of each run, Pallas kernels for 0% -> 0%
where the time goes in v1:
time: 1850 us; the launch traced here: 1840 us
  waiting for transfers between devices  1300 us (70%)
  matrix products  248 us (13%)
  blocking collectives  122 us (7%)
  local copies, waits for them, and re-layouts  98.7 us (5%)
  other arithmetic  48 us (3%)
    unnamed x23, waiting for transfers between devices  329 us
    reduce_scatter x1, waiting for transfers between devices, body(): lax.psum_scatter(grad_down_mat, ('ctx', 'fsdp'), scatter_dimension=0, til...  187 us
    reduce_scatter x1, waiting for transfers between devices, body(): lax.psum_scatter(grad_up_mat, ('ctx', 'fsdp'), scatter_dimension=0, tiled...  187 us
    reduce_scatter x1, waiting for transfers between devices, body(): lax.psum_scatter(grad_out_mat, ('ctx', 'fsdp'), scatter_dimension=0, tile...  142 us
    ppermute x5, waiting for transfers between devices, track_joints(): lax.ppermute(out_arr, comm_axis, tuple(((num, num ^ prior) for num in ran...  86.7 us
    unnamed x2, blocking collectives  82.8 us
    all_gather x2, waiting for transfers between devices, body(): lax.all_gather(keys_mine.reshape(per_device, ctx_rows, width), 'ctx', axi...  74.2 us
    reduce_scatter x2, waiting for transfers between devices, body(): lax.psum_scatter(grad_values_all.astype(jnp.bfloat16), 'ctx', scatter_dim...  62.4 us
  transfers between devices with their start and end apart: 25, of which 21 were waited for; matrix products, arithmetic and copies ran while one was open for 16% of the time, Pallas kernels for 0%

profile of v1, /device:TPU:0, one launch (start us, length us, event | category | flops | bytes accessed | tf_op | source)
XLA Modules:
  0.0 1841.5 jit_solution(10625134275948415095)
XLA Ops:
  16.2 42.3 %all-reduce.18 = (bf16[1024]{0:T(1024)(128)(2,1)S(1)}, bf16[1024]{0:T(1024)(128)(2,1)S(1)}, bf16[1024]{0:T(1024)(128)(2,1)S(1)}, bf16[1024]{0:T(1024)(128)(2,1)S...) all-reduce(bf16[1024]{0:T(1024)(128)(2,1)S(1)} %dynamic-update-slic, ...), channel_id=1, replica_groups=mesh['ctx'=4,'fsdp'=8] {'ctx','fsdp'}, use_global_device_ids=true, to_apply=%add | all-reduce | flops 8192 | bytes 32768
  58.5 11.8 all-gather.16.cloned.1.call-done
  73.7 55.0 %all-gather.20.cloned.1.call-done = bf16[1024,1024]{1,0:T(8,128)(2,1)} async-done(((bf16[32,1024]{1,0:T(8,128)(2,1)}), bf16[1024,1024]{1,0:T(8,128)(2,1)}) %all-gather.20.cloned.1.call-update) | async-done | bytes 2097168 | tf_op jit(solution)/shard_map/all_gather | solution.py:154
  140.6 14.7 collective-permute-done.1
  156.8 49.4 %collective-permute-done.2 = bf16[128,4096]{1,0:T(8,128)(2,1)} collective-permute-done((bf16[128,4096]{1,0:T(8,128)(2,1)S(1)}, bf16[128,4096]{1,0:T(8,128)(2,1)}, u32[]{:S(2)}, u32[]{:S(2)}) %collective-permute-start.2) | collective-permute-done | bytes 1048608 | tf_op jit(solution)/shard_map/ppermute | solution.py:18
  211.4 39.4 %all-gather.4 = bf16[32,1,128]{2,1,0:T(2,128)(2,1)S(1)} all-gather(bf16[1,1,128]{2,1,0:T(2,128)(2,1)S(1)} %bitcast.491), channel_id=1, replica_groups=mesh['ctx'=4,'fsdp'=8] {'ctx','fsdp'}, dimensions={0}, use_global_device_ids=true | all-gather | bytes 8448 | tf_op jit(solution)/shard_map/all_gather | solution.py:162
  252.6 21.4 %collective-permute-done.3 = bf16[256,4096]{1,0:T(8,128)(2,1)} collective-permute-done((bf16[256,4096]{1,0:T(8,128)(2,1)S(1)}, bf16[256,4096]{1,0:T(8,128)(2,1)}, u32[]{:S(2)}, u32[]{:S(2)}) %collective-permute-start.3) | collective-permute-done | bytes 2097184 | tf_op jit(solution)/shard_map/ppermute | solution.py:18
  293.0 38.0 %all-gather.30.cloned.1.call-done = bf16[1024,1024]{1,0:T(8,128)(2,1)} async-done(((bf16[256,1024]{1,0:T(8,128)(2,1)}), bf16[1024,1024]{1,0:T(8,128)(2,1)}) %all-gather.30.cloned.1.call-update) | async-done | bytes 2097168 | tf_op jit(solution)/shard_map/all_gather | solution.py:196
  334.7 26.7 %while.52 = (s32[]{:T(128)}, bf16[4,256,4,64]{1,3,2,0:T(8,128)(2,1)}, f32[4,4,256,1]{2,1,3,0:T(4,128)S(1)}, bf16[4,1024,4,64]{1,3,2,0:T(8,128)(2,1)}, s32[4,256]...) while((s32[]{:T(128)}, ...), condition=%wide.region_6.7_spmd, body=%wide.region_3.6_spmd.sunk | while | flops 281279488 | bytes 19317928 | solution.py:211
  361.5 23.7 %all-gather.32.cloned.1.call-done = bf16[1024,1024]{1,0:T(8,128)(2,1)} async-done(((bf16[256,1024]{1,0:T(8,128)(2,1)}), bf16[1024,1024]{1,0:T(8,128)(2,1)}) %all-gather.32.cloned.1.call-update) | async-done | bytes 2097168 | tf_op jit(solution)/shard_map/all_gather | solution.py:199
  389.1 36.2 %all-gather.34.cloned.1.call-done = bf16[1024,1024]{1,0:T(8,128)(2,1)} async-done(((bf16[256,1024]{1,0:T(8,128)(2,1)}), bf16[1024,1024]{1,0:T(8,128)(2,1)}) %all-gather.34.cloned.1.call-update) | async-done | bytes 2097168 | tf_op jit(solution)/shard_map/all_gather | solution.py:196
  429.1 26.9 %while.53 = (s32[]{:T(128)}, bf16[4,256,4,64]{1,3,2,0:T(8,128)(2,1)}, f32[4,4,256,1]{2,1,3,0:T(4,128)S(1)}, bf16[4,1024,4,64]{1,3,2,0:T(8,128)(2,1)}, s32[4,256]...) while((s32[]{:T(128)}, ...), condition=%wide.region_17.18_spmd, body=%wide.region_14.17_spmd.sunk | while | flops 281279488 | bytes 19317928 | solution.py:211
  456.0 28.8 %all-gather.22.cloned.1.call-done = bf16[1024,1024]{1,0:T(8,128)(2,1)} async-done(((bf16[32,1024]{1,0:T(8,128)(2,1)}), bf16[1024,1024]{1,0:T(8,128)(2,1)}) %all-gather.22.cloned.1.call-update) | async-done | bytes 2097168 | tf_op jit(solution)/shard_map/all_gather | solution.py:157
  489.0 16.2 multiply_convert_fusion.3
  505.3 16.3 multiply_convert_fusion.2
  521.6 42.5 %all-gather.24.cloned.1.call-done = bf16[4096,1024]{1,0:T(8,128)(2,1)} async-done(((bf16[128,1024]{1,0:T(8,128)(2,1)}), bf16[4096,1024]{1,0:T(8,128)(2,1)}) %all-gather.24.cloned.1.call-update) | async-done | bytes 8388624 | tf_op jit(solution)/shard_map/all_gather | solution.py:163
  586.5 56.5 %all-gather.26.cloned.1.call-done = bf16[1024,4096]{1,0:T(8,128)(2,1)} async-done(((bf16[32,4096]{1,0:T(8,128)(2,1)}), bf16[1024,4096]{1,0:T(8,128)(2,1)}) %all-gather.26.cloned.1.call-update) | async-done | bytes 8388624 | tf_op jit(solution)/shard_map/all_gather | solution.py:236
  650.5 11.6 convert_reduce_fusion
  681.4 45.9 %while.54 = (s32[]{:T(128)}, bf16[4,256,4,64]{1,3,2,0:T(8,128)(2,1)S(1)}, bf16[4,1024,4,64]{1,3,2,0:T(8,128)(2,1)}, bf16[4,1024,4,64]{1,3,2,0:T(8,128)(2,1)}, bf...) while((s32[]{:T(128)}, ...), condition=%wide.region_28.29_spmd, body=%wide.region_26.28_spmd.sunk | while | flops 687406080 | bytes 72663312 | solution.py:280
  731.4 46.0 %while.55 = (s32[]{:T(128)}, bf16[4,256,4,64]{1,3,2,0:T(8,128)(2,1)}, bf16[4,1024,4,64]{1,3,2,0:T(8,128)(2,1)}, bf16[4,1024,4,64]{1,3,2,0:T(8,128)(2,1)}, bf16[4...) while((s32[]{:T(128)}, ...), condition=%wide.region_37.38_spmd, body=%wide.region_35.37_spmd.sunk | while | flops 687406080 | bytes 76857680 | solution.py:280
  797.4 14.2 reduce-scatter.21.cloned.1.call-done
  822.0 27.8 %reduce-scatter.19.cloned.1.call-done = bf16[1,256,1024]{1,2,0:T(8,128)(2,1)} async-done(((bf16[1,1024,1024]{1,2,0:T(8,128)(2,1)}), bf16[1,256,1024]{1,2,0:T(8,128)(2,1)}) %reduce-scatter.19.cloned.1.call-update) | async-done | bytes 524304 | tf_op jit(solution)/shard_map/reduce_scatter | solution.py:298
  853.4 34.6 %reduce-scatter.23.cloned.1.call-done = bf16[1,256,1024]{1,2,0:T(8,128)(2,1)} async-done(((bf16[1,1024,1024]{1,2,0:T(8,128)(2,1)}), bf16[1,256,1024]{1,2,0:T(8,128)(2,1)}) %reduce-scatter.23.cloned.1.call-update) | async-done | bytes 524304 | tf_op jit(solution)/shard_map/reduce_scatter | solution.py:298
  903.6 10.0 convolution_add_fusion.1
  918.8 10.1 convolution_add_fusion
  941.9 40.5 %all-reduce.17 = (f32[1024]{0:T(1024)S(1)}, f32[1024]{0:T(1024)S(1)}, f32[1024]{0:T(1024)S(1)}, f32[1024]{0:T(1024)S(1)}, f32[1024]{0:T(1024)S(1)}, /*index=5*/f...) all-reduce(f32[1024]{0:T(1024)S(1)} %reshape.711, ...), channel_id=26, replica_groups=mesh['ctx'=4,'fsdp'=8] {'ctx','fsdp'}, use_global_device_ids=true, to_apply=%region_43.44.clone | all-reduce | flops 12288 | bytes 98304
  994.5 39.2 %reduce-scatter.31.cloned.1.call-done = f32[32,1024]{1,0:T(8,128)} async-done(((f32[1024,1024]{1,0:T(8,128)}), f32[32,1024]{1,0:T(8,128)}) %reduce-scatter.31.cloned.1.call-update) | async-done | bytes 131088
  1033.8 142.1 %reduce-scatter.25.cloned.1.call-done = f32[32,1024]{1,0:T(8,128)} async-done(((f32[1024,1024]{1,0:T(8,128)}), f32[32,1024]{1,0:T(8,128)}) %reduce-scatter.25.cloned.1.call-update) | async-done | bytes 131088 | tf_op jit(solution)/shard_map/reduce_scatter | solution.py:327
  1175.8 142.6 %reduce-scatter.33.cloned.1.call-done = f32[32,1024]{1,0:T(8,128)} async-done(((f32[1024,1024]{1,0:T(8,128)}), f32[32,1024]{1,0:T(8,128)}) %reduce-scatter.33.cloned.1.call-update) | async-done | bytes 131088
  1318.4 142.0 %reduce-scatter.35.cloned.1.call-done = f32[32,1024]{1,0:T(8,128)} async-done(((f32[1024,1024]{1,0:T(8,128)}), f32[32,1024]{1,0:T(8,128)}) %reduce-scatter.35.cloned.1.call-update) | async-done | bytes 131088
  1460.4 187.0 %reduce-scatter.27.cloned.1.call-done = f32[32,4096]{1,0:T(8,128)} async-done(((f32[1024,4096]{1,0:T(8,128)}), f32[32,4096]{1,0:T(8,128)}) %reduce-scatter.27.cloned.1.call-update) | async-done | bytes 524304 | tf_op jit(solution)/shard_map/reduce_scatter | solution.py:331
  1647.4 187.1 %reduce-scatter.29.cloned.1.call-done = f32[128,1024]{1,0:T(8,128)} async-done(((f32[4096,1024]{1,0:T(8,128)}), f32[128,1024]{1,0:T(8,128)}) %reduce-scatter.29.cloned.1.call-update) | async-done | bytes 524304 | tf_op jit(solution)/shard_map/reduce_scatter | solution.py:333
  (615 shorter events, 343.4 us)
Async XLA Ops:
  7.2 121.6 %copy-start.8 = (bf16[2,1,256,1024]{3,2,1,0:T(8,128)(2,1)S(1)}, bf16[2,1,256,1024]{3,2,1,0:T(8,128)(2,1)}, u32[]{:S(2)}) copy-start(bf16[2,1,256,1024]{3,2,1,0:T(8,128)(2,1)} %param.26) | copy-start | bytes 3145732
  7.2 63.0 %all-gather.16.cloned.1.call-start = ((), (), s32[]{:S(2)}) async-start(), calls=%async_computation.10 | async-start | bytes 2162688 | tf_op jit(solution)/shard_map/all_gather | solution.py:155
  7.9 120.8 %all-gather.20.cloned.1.call-start = ((), (), s32[]{:S(2)}) async-start(), calls=%async_computation.12 | async-start | bytes 2162688 | tf_op jit(solution)/shard_map/all_gather | solution.py:154
  8.7 271.6 %all-gather.18.cloned.1.call-start = ((), (), s32[]{:S(2)}) async-start(), calls=%async_computation.11 | async-start | bytes 2162688 | tf_op jit(solution)/shard_map/all_gather | solution.py:152
  9.4 279.7 %all-gather.28.cloned.1.call-start = ((), (), s32[]{:S(2)}) async-start(), calls=%async_computation.20 | async-start | bytes 2621440 | tf_op jit(solution)/shard_map/all_gather | solution.py:199
  73.7 257.3 %all-gather.30.cloned.1.call-start = ((), (), s32[]{:S(2)}) async-start(), calls=%async_computation.21 | async-start | bytes 2621440 | tf_op jit(solution)/shard_map/all_gather | solution.py:196
  131.9 253.2 %all-gather.32.cloned.1.call-start = ((), (), s32[]{:S(2)}) async-start(), calls=%async_computation.22 | async-start | bytes 2621440 | tf_op jit(solution)/shard_map/all_gather | solution.py:199
  133.5 291.8 %all-gather.34.cloned.1.call-start = ((), (), s32[]{:S(2)}) async-start(), calls=%async_computation.23 | async-start | bytes 2621440 | tf_op jit(solution)/shard_map/all_gather | solution.py:196
  136.7 74.7 %copy-start.91 = (bf16[128]{0:T(256)(128)(2,1)S(1)}, bf16[128]{0:T(256)(128)(2,1)}, u32[]{:S(2)}) copy-start(bf16[128]{0:T(256)(128)(2,1)} %param.38) | copy-start | bytes 772
  136.7 114.1 %copy-start.89 = (s32[2,1,4]{2,1,0:T(1,128)S(1)}, s32[2,1,4]{2,1,0:T(1,128)}, u32[]{:S(2)}) copy-start(s32[2,1,4]{2,1,0:T(1,128)} %param.27) | copy-start | bytes 100
  136.7 348.1 %all-gather.22.cloned.1.call-start = ((), (), s32[]{:S(2)}) async-start(), calls=%async_computation.13 | async-start | bytes 2162688 | tf_op jit(solution)/shard_map/all_gather | solution.py:157
  137.5 426.6 %all-gather.24.cloned.1.call-start = ((), (), s32[]{:S(2)}) async-start(), calls=%async_computation.14 | async-start | bytes 8650752 | tf_op jit(solution)/shard_map/all_gather | solution.py:163
  138.2 504.7 %all-gather.26.cloned.1.call-start = ((), (), s32[]{:S(2)}) async-start(), calls=%async_computation.15 | async-start | bytes 8650752 | tf_op jit(solution)/shard_map/all_gather | solution.py:236
  138.3 1.6 collective-permute-start
  140.0 15.3 collective-permute-start.1
  155.5 50.7 %collective-permute-start.2 = (bf16[128,4096]{1,0:T(8,128)(2,1)S(1)}, bf16[128,4096]{1,0:T(8,128)(2,1)}, u32[]{:S(2)}, u32[]{:S(2)}) collective-permute-start(bf16[128,4096]{1,0:T(8,128)(2,1)S(1)} %maximum_select_fusion.5), channel_id=1, source_target_pairs={{0,4},{1,5},{2,6},{3,7},{4,0},{5,1},{6,2},{7,3},{8,12},{9,13},{10,... | collective-permute-start | bytes 3145736 | tf_op jit(solution)/shard_map/ppermute | solution.py:18
  209.2 64.8 %collective-permute-start.3 = (bf16[256,4096]{1,0:T(8,128)(2,1)S(1)}, bf16[256,4096]{1,0:T(8,128)(2,1)}, u32[]{:S(2)}, u32[]{:S(2)}) collective-permute-start(bf16[256,4096]{1,0:T(8,128)(2,1)S(1)} %maximum_select_fusion.2), channel_id=1, source_target_pairs={{0,8},{1,9},{2,10},{3,11},{4,12},{5,13},{6,14},{7,15},{8,0},{9,1},... | collective-permute-start | bytes 6291464 | tf_op jit(solution)/shard_map/ppermute | solution.py:18
  210.7 582.9 %reduce-scatter.17.cloned.1.call-start = ((), (), s32[]{:S(2)}) async-start(), calls=%async_computation.16 | async-start | bytes 2621440 | tf_op jit(solution)/shard_map/reduce_scatter | solution.py:295
  251.2 320.0 %copy-start.58 = (f32[1024]{0:T(1024)}, f32[1024]{0:T(1024)S(1)}, u32[]{:S(2)}) copy-start(f32[1024]{0:T(1024)S(1)} %convert_element_type.386) | copy-start | bytes 12292
  278.7 210.3 %collective-permute-start.4 = (bf16[512,4096]{1,0:T(8,128)(2,1)}, bf16[512,4096]{1,0:T(8,128)(2,1)}, u32[]{:S(2)}, u32[]{:S(2)}) collective-permute-start(bf16[512,4096]{1,0:T(8,128)(2,1)} %maximum_select_fusion.1), channel_id=1, source_target_pairs={{0,16},{1,17},{2,18},{3,19},{4,20},{5,21},{6,22},{7,23},{8,24},{9,... | collective-permute-start | bytes 12582920 | tf_op jit(solution)/shard_map/ppermute | solution.py:18
  488.7 181.9 %copy-start.6 = (f32[256,1024]{1,0:T(8,128)}, f32[256,1024]{1,0:T(8,128)S(1)}, u32[]{:S(2)}) copy-start(f32[256,1024]{1,0:T(8,128)S(1)} %get-tuple-element.451) | copy-start | bytes 3145732
  488.7 181.9 %copy-start.67 = (f32[256]{0:T(256)}, f32[256]{0:T(256)S(1)}, u32[]{:S(2)}) copy-start(f32[256]{0:T(256)S(1)} %broadcast_multiply_fusion.9) | copy-start | bytes 3076
  489.0 181.7 %copy-start.69 = (f32[256]{0:T(256)}, f32[256]{0:T(256)S(1)}, u32[]{:S(2)}) copy-start(f32[256]{0:T(256)S(1)} %add_rsqrt_fusion.1) | copy-start | bytes 3076
  727.3 84.2 %reduce-scatter.21.cloned.1.call-start = ((), (), s32[]{:S(2)}) async-start(), calls=%async_computation.18 | async-start | bytes 2621440 | tf_op jit(solution)/shard_map/reduce_scatter | solution.py:295
  777.5 72.3 %reduce-scatter.19.cloned.1.call-start = ((), (), s32[]{:S(2)}) async-start(), calls=%async_computation.17 | async-start | bytes 2621440 | tf_op jit(solution)/shard_map/reduce_scatter | solution.py:298
  778.2 109.8 %reduce-scatter.23.cloned.1.call-start = ((), (), s32[]{:S(2)}) async-start(), calls=%async_computation.19 | async-start | bytes 2621440 | tf_op jit(solution)/shard_map/reduce_scatter | solution.py:298
  778.8 255.0 %reduce-scatter.31.cloned.1.call-start = ((), (), s32[]{:S(2)}) async-start(), calls=%async_computation.27 | async-start | bytes 4325376
  788.4 387.4 %reduce-scatter.25.cloned.1.call-start = ((), (), s32[]{:S(2)}) async-start(), calls=%async_computation.24 | async-start | bytes 4325376 | tf_op jit(solution)/shard_map/reduce_scatter | solution.py:327
  793.6 524.8 %reduce-scatter.33.cloned.1.call-start = ((), (), s32[]{:S(2)}) async-start(), calls=%async_computation.28 | async-start | bytes 4325376
  821.9 638.5 %reduce-scatter.35.cloned.1.call-start = ((), (), s32[]{:S(2)}) async-start(), calls=%async_computation.29 | async-start | bytes 4325376
  898.5 748.9 %reduce-scatter.27.cloned.1.call-start = ((), (), s32[]{:S(2)}) async-start(), calls=%async_computation.25 | async-start | bytes 17301504 | tf_op jit(solution)/shard_map/reduce_scatter | solution.py:331
  913.6 920.9 %reduce-scatter.29.cloned.1.call-start = ((), (), s32[]{:S(2)}) async-start(), calls=%async_computation.26 | async-start | bytes 17301504 | tf_op jit(solution)/shard_map/reduce_scatter | solution.py:333
  (135 other events, 1114.7 us)
Sparse Core Ops, SparseCore 0:
  11.0 59.1 all-gather.15
  73.2 55.4 all-gather.19
  131.7 97.1 all-gather.17
  231.2 46.5 all-gather.27
  279.4 51.5 all-gather.29
  332.7 52.3 all-gather.31
  387.0 38.2 all-gather.33
  428.3 56.4 all-gather.21
  487.8 76.2 all-gather.23
  566.9 75.9 all-gather.25
  727.5 33.7 reduce-scatter.16
  777.6 33.9 reduce-scatter.20
  814.5 35.1 reduce-scatter.18
  852.8 35.1 reduce-scatter.22
  890.7 142.9 reduce-scatter.30
  1036.5 139.3 reduce-scatter.24
  1178.5 139.8 reduce-scatter.32
  1321.1 139.2 reduce-scatter.34
  1463.2 184.0 reduce-scatter.26
  1650.1 184.3 reduce-scatter.28
